TPU v7x, 256 devices: a whole 4x4x8 slice. The times are simulated.
256 devices in a mesh: grp: 8 (over y, x_hi), tok: 32 (over z, x_lo, core).
Axes of the slice: x: 4 (x_hi: 2, x_lo: 2; x = x_hi * 2 + x_lo), y: 4, z: 8, core: 2. Of those that a mesh axis runs over, the one named last changes fastest.
Arguments:
- layer_input: bfloat16 [8, 6144, 1536], P('grp', 'tok'), may hold values from -54 to 54
- attn_gain: float32 [1536], replicated, may hold values from 0.1 to 1.9
- w_query: bfloat16 [1536, 1536], P('tok'), may hold values from -0.15625 to 0.15625
- w_keyval: bfloat16 [1536, 1024], P('tok'), may hold values from -0.15625 to 0.15625
- w_output: bfloat16 [1536, 1536], P('tok'), may hold values from -0.15625 to 0.15625
- prefix_cache: bfloat16 [8, 512, 1024], P('grp', 'tok'), may hold values from -260 to 260
- lengths: int32 [8, 48], P('grp'), may hold values from 1 to 192, 6144 in all within a row
- moe_gain: float32 [1536], replicated, may hold values from 0.1 to 1.9
- w_router: bfloat16 [1536, 16], replicated, may hold values from -0.15625 to 0.15625
- routes: int32 [8, 6144, 2], P('grp', 'tok'), may hold values from 0 to 15, all different within a row; in each aligned block of 192 rows (0 to 191, 192 to 383, ..., all dimensions but the last counted through in order) at most 30 rows name the same one
- w_expert_in: bfloat16 [32, 1536, 1024], P('tok', 'grp'), may hold values from -0.15625 to 0.15625
- w_expert_out: bfloat16 [32, 512, 1536], P('tok', 'grp'), may hold values from -0.1875 to 0.1875
Outputs:
- hidden: bfloat16 [8, 6144, 1536], P('grp', 'tok')
- suffix_cache: bfloat16 [8, 6144, 1024], P('grp', 'tok')
Inputs may be any that keep to these rules, and one draw needn't show every extreme that they name: `lengths`: each row sums to 6144, and its largest length is 192. A token's 2 routes differ. Among the rows of one device no expert is named more than 30 times, a bound that some block reaches in some devices' rows.
All inputs are finite; a program needn't handle non-finite values.
Results may differ from a plain program's by a relative error of at most 0.0073.
The roundings to bfloat16 on the way count: a program that leaves them out, or rounds other values in their place, can miss the bound.
Values may be sent and summed in bfloat16 or wider, within the bound.
A program may use at most 64 MiB of HBM per device.

v0:
```python
import jax
import jax.numpy as jnp
from jax import lax
from jax.sharding import PartitionSpec as P

HEADS = 24
KV_HEADS = 8
HEAD_DIM = 64
TOP = 2


EPS = 1e-05


def passed_along(value, axis, steps):
    count = lax.axis_size(axis)
    initial, last = (max(0, -steps), min(count, count - steps))
    return lax.ppermute(value, axis, [(source, source + steps) for source in range(initial, last)])


def rms_scale(inputs, scale_row):
    inputs = inputs.astype(jnp.float32)
    inverse = lax.rsqrt(jnp.mean(inputs * inputs, axis=-1, keepdims=True) + EPS)
    return inputs * inverse * scale_row


def segment_of(req_lengths, positions):
    request_ends = jnp.cumsum(req_lengths, dtype=jnp.int32)
    return jnp.sum((request_ends[None, :] <= positions[:, None]).astype(jnp.int32), axis=1)


def product(left, right):
    return jnp.dot(left, right, preferred_element_type=jnp.float32)


def attend(soft_state, queries, key_block, allowed):
    maxima, totals, numerators = soft_state
    kv_width = key_block.shape[1] // 2
    key_rows = key_block[:, :kv_width].reshape(
        key_block.shape[0], queries.shape[1], queries.shape[3]
    )
    value_rows = key_block[:, kv_width:].reshape(
        key_block.shape[0], queries.shape[1], queries.shape[3]
    )
    scores = jnp.einsum(
        "tkgd,skd->tkgs", queries, key_rows, preferred_element_type=jnp.float32
    ) * queries.shape[3] ** (-0.5)
    if allowed is not None:
        scores = jnp.where(allowed[:, None, None, :], scores, -jnp.inf)
    new_max = jnp.maximum(maxima, jnp.max(scores, axis=-1))
    rescale = jnp.exp(maxima - new_max)
    weights = jnp.exp(scores - new_max[..., None])
    totals = totals * rescale + jnp.sum(weights, axis=-1)
    numerators = numerators * rescale[..., None] + jnp.einsum(
        "tkgs,skd->tkgd",
        weights.astype(jnp.bfloat16),
        value_rows,
        preferred_element_type=jnp.float32,
    )
    return (new_max, totals, numerators)


def on_device(
    layer_input,
    attn_gain,
    w_query,
    w_keyval,
    w_output,
    prefix_cache,
    lengths,
    moe_gain,
    w_router,
    routes,
    w_expert_in,
    w_expert_out,
):
    tokens = layer_input[0]
    row_count = tokens.shape[0]
    model_width = tokens.shape[1]
    group_share = HEADS // KV_HEADS
    normed = rms_scale(tokens, attn_gain).astype(jnp.bfloat16)
    columns = normed
    query_full = product(columns, lax.all_gather(w_query, "tok", axis=0, tiled=True))
    keyval_full = product(columns, lax.all_gather(w_keyval, "tok", axis=0, tiled=True))
    queries = query_full.astype(jnp.bfloat16).reshape(row_count, KV_HEADS, group_share, HEAD_DIM)
    keyval = keyval_full.astype(jnp.bfloat16)
    position = lax.axis_index("tok")
    positions = position * row_count + jnp.arange(row_count, dtype=jnp.int32)
    req_lengths = lengths[0]
    own_seg = segment_of(req_lengths, positions)
    before_seg = jnp.where(
        positions >= row_count, segment_of(req_lengths, positions - row_count), -1
    )
    earlier = passed_along(keyval, "tok", 1)
    near_block = jnp.concatenate([earlier, keyval], axis=0)
    near_seg = jnp.concatenate([before_seg, own_seg])
    near_pos = jnp.concatenate([positions - row_count, positions])
    allowed = (near_seg[None, :] == own_seg[:, None]) & (near_pos[None, :] <= positions[:, None])
    soft_state = (
        jnp.full((row_count, KV_HEADS, group_share), -jnp.inf, jnp.float32),
        jnp.zeros((row_count, KV_HEADS, group_share), jnp.float32),
        jnp.zeros((row_count, KV_HEADS, group_share, HEAD_DIM), jnp.float32),
    )
    soft_state = attend(soft_state, queries, near_block, allowed)
    prefix_whole = lax.all_gather(prefix_cache[0], "tok", axis=0, tiled=True)
    maxima, totals, numerators = attend(soft_state, queries, prefix_whole, None)
    attended = (
        (numerators / totals[..., None]).astype(jnp.bfloat16).reshape(row_count, HEADS * HEAD_DIM)
    )
    columns = attended
    residual = tokens.astype(jnp.float32) + product(
        columns, lax.all_gather(w_output, "tok", axis=0, tiled=True)
    )
    normed2 = rms_scale(residual, moe_gain).astype(jnp.bfloat16)
    logits = product(normed2, w_router)
    experts = w_router.shape[1]
    chosen = routes[0]
    expert_marks = chosen[:, :, None] == jnp.arange(experts, dtype=jnp.int32)
    picked = jnp.sum(jnp.where(expert_marks, logits[:, None, :], 0.0), axis=-1)
    scores = jax.nn.sigmoid(picked)
    gate_weights = scores / jnp.sum(scores, axis=-1, keepdims=True)
    capacity = max(4, 5 * row_count * TOP // (4 * experts))
    flat_routes = chosen.reshape(-1)
    flat_marks = expert_marks.reshape(-1, experts).astype(jnp.int32)
    prior_count = jnp.cumsum(flat_marks, axis=0, dtype=jnp.int32) - flat_marks
    slot_index = jnp.sum(prior_count * flat_marks, axis=1)
    target = flat_routes * capacity + slot_index
    copies = flat_routes.shape[0]
    slot_match = target[None, :] == jnp.arange(experts * capacity, dtype=jnp.int32)[:, None]
    filled = jnp.any(slot_match, axis=1)
    source = jnp.sum(jnp.where(slot_match, jnp.arange(copies, dtype=jnp.int32)[None, :], 0), axis=1)
    outgoing = jnp.where(filled[:, None], normed2[source // TOP], 0).reshape(
        experts, capacity, model_width
    )
    to_send = jnp.repeat(outgoing, 2, axis=0)
    arrived = lax.all_to_all(to_send, "tok", split_axis=0, concat_axis=0, tiled=True)
    flat_rows = arrived.reshape(-1, model_width)
    columns = flat_rows
    gate_up = product(columns, lax.all_gather(w_expert_in[0], "grp", axis=0, tiled=True))
    half_units = gate_up.shape[1] // 2
    act = (jax.nn.silu(gate_up[:, :half_units]) * gate_up[:, half_units:]).astype(jnp.bfloat16)
    columns = act
    partial_out = product(columns, lax.all_gather(w_expert_out[0], "grp", axis=0, tiled=True))
    returned = lax.all_to_all(
        partial_out.reshape(arrived.shape).astype(jnp.bfloat16),
        "tok",
        split_axis=0,
        concat_axis=0,
        tiled=True,
    ).astype(jnp.float32)
    results = jnp.sum(returned.reshape(experts, 2, capacity, model_width), axis=1).astype(
        jnp.bfloat16
    )
    gathered = results.reshape(experts * capacity, model_width)[target].astype(jnp.float32)
    weighted = jnp.sum(
        gathered.reshape(row_count, TOP, model_width) * gate_weights[:, :, None], axis=1
    )
    hidden = (residual + weighted).astype(jnp.bfloat16)
    return (hidden[None], keyval[None])


def solution(mesh):
    in_specs = (
        P("grp", "tok", None),
        P(),
        P("tok", None),
        P("tok", None),
        P("tok", None),
        P("grp", "tok", None),
        P("grp", None),
        P(),
        P(),
        P("grp", "tok", None),
        P("tok", "grp", None),
        P("tok", "grp", None),
    )
    out_specs = (P("grp", "tok", None), P("grp", "tok", None))
    return jax.shard_map(
        on_device, mesh=mesh, in_specs=in_specs, out_specs=out_specs, check_vma=False
    )
```

profile of v0, /device:TPU:1, one launch (start us, length us, event | category | flops | bytes accessed | tf_op | source)
XLA Modules:
  0.0 535.8 jit_solution(8123321330734562649)
XLA Ops:
  7.2 0.7 all-gather.10.cloned.1.call-update
  8.0 0.7 all-gather.16.cloned.1.call-update
  8.7 0.7 all-gather.12.cloned.1.call-update
  9.4 0.5 all-gather.14.cloned.1.call-update
  10.0 0.5 all-gather.18.cloned.1.call-update
  10.6 0.8 copy.41
  11.4 0.1 reshape_squeeze.3
  11.5 0.1 eq.68
  11.7 1.3 fusion.22
  13.0 0.7 copy.35
  13.8 0.1 reduce.1
  13.9 0.1 convert_reduce_fusion.1
  14.0 0.9 reduce-window.19
  14.9 0.2 slice_reduce_fusion
  15.2 0.2 select_reduce_fusion
  15.5 0.1 compare_and_fusion
  15.7 63.8 %all-gather.10.cloned.1.call-done = bf16[1536,1024]{1,0:T(8,128)(2,1)} async-done(((bf16[48,1024]{1,0:T(8,128)(2,1)}), bf16[1536,1024]{1,0:T(8,128)(2,1)}) %all-gather.10.cloned.1.call-update) | async-done | bytes 3145744 | tf_op jit(solution)/shard_map/all_gather | solution.py:84
  79.5 2.9 convolution_convert_fusion.2
  82.4 2.7 collective-permute-start
  85.2 0.2 fusion.27
  85.4 59.2 %all-gather.16.cloned.1.call-done = bf16[1,512,1024]{2,1,0:T(8,128)(2,1)} async-done(((bf16[1,16,1024]{2,1,0:T(8,128)(2,1)}), bf16[1,512,1024]{2,1,0:T(8,128)(2,1)}) %all-gather.16.cloned.1.call-update) | async-done | bytes 1048592 | tf_op jit(solution)/shard_map/all_gather | solution.py:105
  144.6 1.3 fusion.42
  145.9 0.2 copy.40
  146.2 0.2 copy.39
  146.5 0.2 copy.36
  146.7 0.9 copy.38
  147.6 65.7 %all-gather.12.cloned.1.call-done = bf16[1536,1536]{1,0:T(8,128)(2,1)} async-done(((bf16[48,1536]{1,0:T(8,128)(2,1)}), bf16[1536,1536]{1,0:T(8,128)(2,1)}) %all-gather.12.cloned.1.call-update) | async-done | bytes 4718608 | tf_op jit(solution)/shard_map/all_gather | solution.py:83
  213.3 3.5 convolution_convert_fusion.1
  216.8 0.3 copy.37
  217.1 1.6 bitcast_reduce_fusion
  218.7 1.7 fusion.5
  220.3 2.4 fusion.1
  222.7 3.2 fusion.6
  226.0 2.3 fusion.3
  228.3 2.5 fusion.18
  230.8 51.3 %all-gather.14.cloned.1.call-done = bf16[1536,1536]{1,0:T(8,128)(2,1)} async-done(((bf16[48,1536]{1,0:T(8,128)(2,1)}), bf16[1536,1536]{1,0:T(8,128)(2,1)}) %all-gather.14.cloned.1.call-update) | async-done | bytes 4718608 | tf_op jit(solution)/shard_map/all_gather | solution.py:112
  282.1 3.6 multiply_reduce_fusion.1
  285.7 1.1 copy-done.1
  286.8 0.2 multiply_convert_fusion
  286.9 2.9 gather_fusion
  289.9 1.5 gather.9
  291.4 0.2 broadcast_select_fusion
  291.6 2.1 broadcast_in_dim.108
  293.7 6.4 %all-to-all-start = ((bf16[32,30,1536]{2,1,0:T(8,128)(2,1)}), bf16[32,30,1536]{2,1,0:T(8,128)(2,1)}, u32[]{:S(2)}, u32[]{:S(2)}) async-start(bf16[32,30,1536]{2,1,0:T(8,128)(2,1)} %bitcast.112), calls=%async_computation | async-start | bytes 6291456 | tf_op jit(solution)/shard_map/all_to_all | solution.py:136
  300.1 0.2 all-gather.20.cloned.1.call-start
  300.3 0.3 all-gather.20.cloned.1.call-update
  300.7 71.3 %all-to-all-done = bf16[32,30,1536]{2,1,0:T(8,128)(2,1)} async-done(((bf16[32,30,1536]{2,1,0:T(8,128)(2,1)}), bf16[32,30,1536]{2,1,0:T(8,128)(2,1)}, u32[]{:S(2)}, u32[]{:S(2)}) %all-to-all-start) | async-done | bytes 2949152 | tf_op jit(solution)/shard_map/all_to_all | solution.py:136
  372.0 4.4 reshape.322
  376.4 7.9 %fusion.13 = f32[960,1024]{1,0:T(8,128)} fusion(bf16[960,1536]{1,0:T(8,128)(2,1)} %reshape.322, bf16[1,1536,1024]{2,1,0:T(8,128)(2,1)} %all-gather.18.cloned.1.call-done), kind=kOutput, calls=%fused_computation.19 | convolution fusion | flops 3019898880 | bytes 10027008 | tf_op jit(solution)/shard_map/dot_general | solution.py:33
  384.3 40.2 %all-gather.20.cloned.1.call-done = bf16[1,512,1536]{2,1,0:T(8,128)(2,1)} async-done(((bf16[1,64,1536]{2,1,0:T(8,128)(2,1)}), bf16[1,512,1536]{2,1,0:T(8,128)(2,1)}) %all-gather.20.cloned.1.call-update) | async-done | bytes 1572880 | tf_op jit(solution)/shard_map/all_gather | solution.py:143
  424.5 5.9 %convolution_convert_fusion = bf16[960,1536]{1,0:T(8,128)(2,1)} fusion(bf16[1,512,1536]{2,1,0:T(8,128)(2,1)} %all-gather.20.cloned.1.call-done, f32[960,1024]{1,0:T(8,128)} %fusion.13), kind=kOutput, calls=%fused_computation.15 | convolution fusion | flops 1514373120 | bytes 8454144 | tf_op jit(solution)/shard_map/dot_general | solution.py:33
  430.5 4.5 convert_element_type.85
  434.9 9.0 %all-to-all-start.1 = ((bf16[32,30,1536]{2,1,0:T(8,128)(2,1)}), bf16[32,30,1536]{2,1,0:T(8,128)(2,1)}, u32[]{:S(2)}, u32[]{:S(2)}) async-start(bf16[32,30,1536]{2,1,0:T(8,128)(2,1)} %convert_element_type.85), calls=%async_computation.1 | async-start | bytes 6291456 | tf_op jit(solution)/shard_map/all_to_all | solution.py:144
  443.9 0.1 copy.44
  444.0 0.1 mul.149
  444.2 0.2 fusion.43
  444.6 0.1 copy.45
  444.7 71.1 %all-to-all-done.1 = bf16[32,30,1536]{2,1,0:T(8,128)(2,1)} async-done(((bf16[32,30,1536]{2,1,0:T(8,128)(2,1)}), bf16[32,30,1536]{2,1,0:T(8,128)(2,1)}, u32[]{:S(2)}, u32[]{:S(2)}) %all-to-all-start.1) | async-done | bytes 2949152 | tf_op jit(solution)/shard_map/all_to_all | solution.py:144
  515.8 2.5 bitcast_reduce_fusion.1
  518.3 0.4 convert_element_type.87
  518.7 2.8 gather_fusion.1
  521.5 2.8 reshape.326
  524.4 3.6 multiply_reduce_fusion
  528.0 0.9 fusion.28
  (47 shorter events, 0.9 us)
Async XLA Ops:
  7.2 437.1 %copy-start = (bf16[1536,16]{0,1:T(8,128)(2,1)S(1)}, bf16[1536,16]{0,1:T(8,128)(2,1)}, u32[]{:S(2)}) copy-start(bf16[1536,16]{0,1:T(8,128)(2,1)} %param.20) | copy-start | bytes 147460
  7.2 72.3 %all-gather.10.cloned.1.call-start = ((), (), s32[]{:S(2)}) async-start(), calls=%async_computation.2 | async-start | bytes 3244032 | tf_op jit(solution)/shard_map/all_gather | solution.py:84
  7.9 136.7 %all-gather.16.cloned.1.call-start = ((), (), s32[]{:S(2)}) async-start(), calls=%async_computation.5 | async-start | bytes 1081344 | tf_op jit(solution)/shard_map/all_gather | solution.py:105
  8.7 204.6 %all-gather.12.cloned.1.call-start = ((), (), s32[]{:S(2)}) async-start(), calls=%async_computation.3 | async-start | bytes 4866048 | tf_op jit(solution)/shard_map/all_gather | solution.py:83
  9.4 272.7 %all-gather.14.cloned.1.call-start = ((), (), s32[]{:S(2)}) async-start(), calls=%async_computation.4 | async-start | bytes 4866048 | tf_op jit(solution)/shard_map/all_gather | solution.py:112
  10.0 366.5 %all-gather.18.cloned.1.call-start = ((), (), s32[]{:S(2)}) async-start(), calls=%async_computation.6 | async-start | bytes 3538944 | tf_op jit(solution)/shard_map/all_gather | solution.py:139
  82.4 64.1 %copy-start.5 = (bf16[192,1024]{1,0:T(8,128)(2,1)}, bf16[192,1024]{1,0:T(8,128)(2,1)S(1)}, u32[]{:S(2)}) copy-start(bf16[192,1024]{1,0:T(8,128)(2,1)S(1)} %convolution_convert_fusion.2) | copy-start | bytes 1179652
  82.4 64.0 %collective-permute-start = (bf16[192,1024]{1,0:T(8,128)(2,1)S(1)}, bf16[192,1024]{1,0:T(8,128)(2,1)S(1)}, u32[]{:S(2)}, u32[]{:S(2)}) collective-permute-start(bf16[192,1024]{1,0:T(8,128)(2,1)S(1)} %convolution_convert_fusion.2), channel_id=1, source_target_pairs={{0,1},{1,2},{2,3},{3,4},{4,5},{5,6},{6,7},{7,8},{8,9},{9,10},{10,1... | collective-permute-start | bytes 1179656 | tf_op jit(solution)/shard_map/ppermute | solution.py:18
  145.9 67.4 %copy-start.3 = (bf16[1,192,1536]{2,1,0:T(8,128)(2,1)S(1)}, bf16[1,192,1536]{2,1,0:T(8,128)(2,1)}, u32[]{:S(2)}) copy-start(bf16[1,192,1536]{2,1,0:T(8,128)(2,1)} %param.12) | copy-start | bytes 1769476
  145.9 67.4 %copy-start.8 = (f32[1536]{0:T(1024)S(1)}, f32[1536]{0:T(1024)}, u32[]{:S(2)}) copy-start(f32[1536]{0:T(1024)} %param.13) | copy-start | bytes 18436
  226.0 2.3 copy-start.4
  282.1 4.7 copy-start.7
  285.7 1.1 copy-start.1
  293.7 78.3 %all-to-all-start = ((bf16[32,30,1536]{2,1,0:T(8,128)(2,1)}), bf16[32,30,1536]{2,1,0:T(8,128)(2,1)}, u32[]{:S(2)}, u32[]{:S(2)}) async-start(bf16[32,30,1536]{2,1,0:T(8,128)(2,1)} %bitcast.112), calls=%async_computation | async-start | bytes 6291456 | tf_op jit(solution)/shard_map/all_to_all | solution.py:136
  300.1 124.4 %all-gather.20.cloned.1.call-start = ((), (), s32[]{:S(2)}) async-start(), calls=%async_computation.7 | async-start | bytes 1769472 | tf_op jit(solution)/shard_map/all_gather | solution.py:143
  434.9 9.0 %copy-start.6 = (s32[1,192,2]{1,2,0:T(2,128)S(1)}, s32[1,192,2]{1,2,0:T(2,128)}, u32[]{:S(2)}) copy-start(s32[1,192,2]{1,2,0:T(2,128)} %param.21) | copy-start | bytes 4612
  434.9 80.9 %all-to-all-start.1 = ((bf16[32,30,1536]{2,1,0:T(8,128)(2,1)}), bf16[32,30,1536]{2,1,0:T(8,128)(2,1)}, u32[]{:S(2)}, u32[]{:S(2)}) async-start(bf16[32,30,1536]{2,1,0:T(8,128)(2,1)} %convert_element_type.85), calls=%async_computation.1 | async-start | bytes 6291456 | tf_op jit(solution)/shard_map/all_to_all | solution.py:144
  524.4 3.6 copy-start.2
Sparse Core Ops, SparseCore 0:
  9.8 69.5 all-gather.9
  81.3 63.2 all-gather.15
  146.5 66.7 all-gather.11
  215.0 67.0 all-gather.13
  284.5 88.3 all-gather.17
  375.4 49.0 all-gather.19
where the time goes:
time: 536 us
  waiting for transfers between devices  426 us (79%)
  matrix products  33 us (6%)
  local copies, waits for them, and re-layouts  28.2 us (5%)
  starting transfers between devices  18.5 us (3%)
  other arithmetic  15.3 us (3%)
  between operations  14.5 us (3%)
    all_to_all x1, waiting for transfers between devices, on_device(): lax.all_to_all(to_send, 'tok', split_axis=0, concat_axis=0, tiled=True)  71.3 us
    all_to_all x1, waiting for transfers between devices, on_device(): lax.all_to_all(partial_out.reshape(arrived.shape).astype(jnp.bfloat16), '...  71.1 us
    all_gather x1, waiting for transfers between devices, on_device(): lax.all_gather(w_query, 'tok', axis=0, tiled=True)  65.7 us
    all_gather x1, waiting for transfers between devices, on_device(): lax.all_gather(w_keyval, 'tok', axis=0, tiled=True)  63.8 us
    all_gather x1, waiting for transfers between devices, on_device(): prefix_whole = lax.all_gather(prefix_cache[0], 'tok', axis=0, tiled=True)  59.2 us
    all_gather x1, waiting for transfers between devices, on_device(): lax.all_gather(w_output, 'tok', axis=0, tiled=True)  51.3 us
    all_gather x1, waiting for transfers between devices, on_device(): lax.all_gather(w_expert_out[0], 'grp', axis=0, tiled=True)  40.2 us
    dot_general x6, matrix products, product(): return jnp.dot(left, right, preferred_element_type=jnp.float32)  24 us
  transfers between devices with their start and end apart: 9, of which 7 were waited for; matrix products, arithmetic and copies ran while one was open for 10% of the time, Pallas kernels for 0%

commit v1 on v0

--- a/solution.py
+++ b/solution.py
@@ -1,7 +1,14 @@
 import jax
 import jax.numpy as jnp
 from jax import lax
+from jax.experimental import pallas as pl
+from jax.experimental.pallas import tpu as pltpu
 from jax.sharding import PartitionSpec as P
+
+MESH = pl.DeviceIdType.MESH
+Z, Y, X = 8, 4, 4
+SLOTS = 32
+N_COPIES = 160
 
 HEADS = 24
 KV_HEADS = 8
@@ -31,6 +38,272 @@
 
 def product(left, right):
     return jnp.dot(left, right, preferred_element_type=jnp.float32)
+
+
+def greet(devices):
+    barrier = pltpu.get_barrier_semaphore()
+    for device in devices:
+        pl.semaphore_signal(barrier, inc=1, device_id=device, device_id_type=MESH)
+    pl.semaphore_wait(barrier, len(devices))
+
+
+def gather_kernel(
+    qkv, wo, pre, win, wout,
+    qkv_all, wo_all, pre_all, win_own, win_other, wout_own, wout_other,
+    relay_in, relay_out, send, recv, local,
+):
+    g, t = lax.axis_index("grp"), lax.axis_index("tok")
+    y, xh = g // 2, g % 2
+    z, xl, core = t // 4, (t // 2) % 2, t % 2
+    x = xh * 2 + xl
+
+    def at_x(step):
+        nx = (x + step + X) % X
+        return (y * 2 + nx // 2, z * 4 + (nx % 2) * 2 + core)
+
+    def at_z(step):
+        return (g, ((z + step + Z) % Z) * 4 + xl * 2 + core)
+
+    def at_y(step):
+        return (((y + step + Y) % Y) * 2 + xh, t)
+
+    x_up, x_down = at_x(1), at_x(-1)
+    z_up, z_down, y_up, y_down = at_z(1), at_z(-1), at_y(1), at_y(-1)
+    mate = (g, z * 4 + xl * 2 + 1 - core)
+    pair = (g, z * 4 + (1 - xl) * 2 + core)
+
+    def tok_at(dz, parity, other_core=0):
+        lane = (1 - xl) if parity else xl
+        side = (1 - core) if other_core else core
+        return ((z + dz + Z) % Z) * 4 + lane * 2 + side
+
+    def grp_at(dy, across):
+        return ((y + dy + Y) % Y) * 2 + ((1 - xh) if across else xh)
+
+    slots, sends = {}, []
+
+    def start(name, src, dst, device):
+        slots[name] = len(slots)
+        copy = pltpu.make_async_remote_copy(
+            src_ref=src, dst_ref=dst, send_sem=send.at[slots[name]],
+            recv_sem=recv.at[slots[name]], device_id=device, device_id_type=MESH,
+        )
+        copy.start()
+        sends.append(copy)
+
+    def arrived(name, dst):
+        pltpu.make_async_remote_copy(
+            src_ref=dst, dst_ref=dst, send_sem=send.at[slots[name]],
+            recv_sem=recv.at[slots[name]], device_id=mate, device_id_type=MESH,
+        ).wait_recv()
+
+    greet([x_up, x_down, z_up, z_down, y_up, y_down, mate])
+
+    own = []
+    for src, dst in (
+        (qkv, qkv_all.at[t]), (wo, wo_all.at[t]), (pre, pre_all.at[t]),
+        (win, win_own.at[g]), (wout, wout_own.at[g]),
+    ):
+        own.append(pltpu.make_async_copy(src, dst, local.at[len(own)]))
+        own[-1].start()
+
+    def along_z(k, src_up, src_down):
+        up, down = tok_at(1 - k, 0), tok_at(k - 1, 0)
+        start(("up", "pre", k), src_up[2], pre_all.at[up], z_up)
+        start(("up", "qkv", k), src_up[0], qkv_all.at[up], z_up)
+        if k < 4:
+            start(("up", "wo", k), src_up[1], wo_all.at[up], z_up)
+            start(("down", "pre", k), src_down[2], pre_all.at[down], z_down)
+            start(("down", "qkv", k), src_down[0], qkv_all.at[down], z_down)
+        start(("down", "wo", k), src_down[1], wo_all.at[down], z_down)
+
+    def to_mate(dz, parity, src):
+        at = tok_at(dz, parity)
+        start(("mate", "qkv", dz, parity), src[0], qkv_all.at[at], mate)
+        start(("mate", "wo", dz, parity), src[1], wo_all.at[at], mate)
+        start(("mate", "pre", dz, parity), src[2], pre_all.at[at], mate)
+
+    def along_x(dz, src):
+        at = tok_at(dz, 0)
+        start(("x", "pre", dz), src[2], pre_all.at[at], pair)
+        start(("x", "qkv", dz), src[0], qkv_all.at[at], x_up)
+        start(("x", "wo", dz), src[1], wo_all.at[at], x_down)
+        to_mate(dz, 0, src)
+
+    def held(at):
+        return (qkv_all.at[at], wo_all.at[at], pre_all.at[at])
+
+    def from_x(dz):
+        at = tok_at(dz, 1)
+        for name, ref in (("pre", pre_all), ("qkv", qkv_all), ("wo", wo_all)):
+            arrived(("x", name, dz), ref.at[at])
+        to_mate(dz, 1, held(at))
+
+    def expert_mate(dy, across, src):
+        at = grp_at(dy, across)
+        start(("mate", "win", dy, across), src[0], win_other.at[at], mate)
+        start(("mate", "wout", dy, across), src[1], wout_other.at[at], mate)
+
+    def along_y(across, src):
+        at = grp_at(0, across)
+        for way, device in (("yup", y_up), ("ydown", y_down)):
+            start((way, "win", across), src[0], win_own.at[at], device)
+            start((way, "wout", across), src[1], wout_own.at[at], device)
+        expert_mate(0, across, src)
+
+    def expert_held(at):
+        return (win_own.at[at], wout_own.at[at])
+
+    part = 144
+
+    def from_y(across):
+        at = grp_at(-1, across)
+        arrived(("yup", "win", across), win_own.at[at])
+        start(("yup2", "win", across), win_own.at[at, pl.ds(0, part)],
+              win_own.at[at, pl.ds(0, part)], y_up)
+        arrived(("yup", "wout", across), wout_own.at[at])
+        expert_mate(-1, across, expert_held(at))
+        at = grp_at(1, across)
+        rest = 192 - part
+        arrived(("ydown", "win", across), win_own.at[at])
+        start(("ydown2", "win", across), win_own.at[at, pl.ds(part, rest)],
+              win_own.at[at, pl.ds(part, rest)], y_down)
+        arrived(("ydown", "wout", across), wout_own.at[at])
+        start(("ydown2", "wout", across), wout_own.at[at], wout_own.at[at], y_down)
+        expert_mate(1, across, expert_held(at))
+
+    def from_y_far(across):
+        at = grp_at(2, across)
+        arrived(("yup2", "win", across), win_own.at[at, pl.ds(0, part)])
+        arrived(("ydown2", "win", across), win_own.at[at, pl.ds(part, 192 - part)])
+        arrived(("ydown2", "wout", across), wout_own.at[at])
+        expert_mate(2, across, expert_held(at))
+
+    mine = (qkv, wo, pre)
+    along_z(1, mine, mine)
+    start(("relay", "win"), win, relay_in, x_down)
+    start(("relay", "wout"), wout, relay_out, x_down)
+    along_y(0, (win, wout))
+    along_x(0, mine)
+
+    for k in (1, 2, 3):
+        for name, ref in (("pre", pre_all), ("qkv", qkv_all), ("wo", wo_all)):
+            arrived(("up", name, k), ref.at[tok_at(-k, 0)])
+            arrived(("down", name, k), ref.at[tok_at(k, 0)])
+        along_z(k + 1, held(tok_at(-k, 0)), held(tok_at(k, 0)))
+        along_x(-k, held(tok_at(-k, 0)))
+        along_x(k, held(tok_at(k, 0)))
+        if k == 1:
+            next_at = ((x + 1) % X) // 2 + y * 2
+            arrived(("relay", "win"), relay_in)
+            start(("relay2", "win"), relay_in, win_own.at[next_at], x_down)
+            arrived(("relay", "wout"), relay_out)
+            start(("relay2", "wout"), relay_out, wout_own.at[next_at], x_down)
+            from_x(0)
+            from_y(0)
+        if k == 2:
+            from_x(-1)
+            from_x(1)
+            from_y_far(0)
+        if k == 3:
+            across_at = grp_at(0, 1)
+            arrived(("relay2", "win"), win_own.at[across_at])
+            arrived(("relay2", "wout"), wout_own.at[across_at])
+            along_y(1, expert_held(across_at))
+            from_x(-2)
+            from_x(2)
+
+    at = tok_at(4, 0)
+    arrived(("up", "pre", 4), pre_all.at[at])
+    arrived(("up", "qkv", 4), qkv_all.at[at])
+    arrived(("down", "wo", 4), wo_all.at[at])
+    along_x(4, held(at))
+    from_x(-3)
+    from_x(3)
+    from_y(1)
+    from_x(4)
+    from_y_far(1)
+
+    for dz in (0, -1, 1, -2, 2, -3, 3, 4):
+        for parity in (0, 1):
+            at = tok_at(dz, parity, 1)
+            for name, ref in (("pre", pre_all), ("qkv", qkv_all), ("wo", wo_all)):
+                arrived(("mate", name, dz, parity), ref.at[at])
+    for dy in (0, -1, 1, 2):
+        for across in (0, 1):
+            at = grp_at(dy, across)
+            arrived(("mate", "win", dy, across), win_other.at[at])
+            arrived(("mate", "wout", dy, across), wout_other.at[at])
+    for copy in own:
+        copy.wait()
+    for copy in sends:
+        copy.wait_send()
+
+
+def gather_all(qkv, wo, pre, win, wout):
+    dtype = jnp.bfloat16
+    tok, grp = lax.axis_size("tok"), lax.axis_size("grp")
+    shapes = [(tok,) + a.shape for a in (qkv, wo, pre)]
+    shapes += [(grp,) + win.shape] * 2 + [(grp,) + wout.shape] * 2
+    return pl.pallas_call(
+        gather_kernel,
+        out_shape=[jax.ShapeDtypeStruct(shape, dtype) for shape in shapes],
+        in_specs=[pl.BlockSpec(memory_space=pltpu.VMEM)] * 5,
+        out_specs=[pl.BlockSpec(memory_space=pl.ANY)] * 7,
+        scratch_shapes=[
+            pltpu.VMEM(win.shape, dtype),
+            pltpu.VMEM(wout.shape, dtype),
+            pltpu.SemaphoreType.DMA((N_COPIES,)),
+            pltpu.SemaphoreType.DMA((N_COPIES,)),
+            pltpu.SemaphoreType.DMA((5,)),
+        ],
+        compiler_params=pltpu.CompilerParams(collective_id=0, has_side_effects=True),
+    )(qkv, wo, pre, win, wout)
+
+
+def exchange_kernel(rows, got, send, recv, local):
+    g, t = lax.axis_index("grp"), lax.axis_index("tok")
+    chip, core = t // 2, t % 2
+    chips = rows.shape[0]
+    others = [(chip + step) % chips for step in range(1, chips)]
+    greet([(g, other * 2 + core) for other in others])
+    keep = pltpu.make_async_copy(rows.at[chip], got.at[chip], local)
+    keep.start()
+    copies = []
+    for n, other in enumerate(others):
+        copy = pltpu.make_async_remote_copy(
+            src_ref=rows.at[other], dst_ref=got.at[chip], send_sem=send.at[n],
+            recv_sem=recv.at[n], device_id=(g, other * 2 + core), device_id_type=MESH,
+        )
+        copy.start()
+        copies.append(copy)
+    for n in range(chips - 1):
+        source = (chip + chips - 1 - n) % chips
+        pltpu.make_async_remote_copy(
+            src_ref=got.at[source], dst_ref=got.at[source], send_sem=send.at[n],
+            recv_sem=recv.at[n], device_id=(g, others[n] * 2 + core), device_id_type=MESH,
+        ).wait_recv()
+    for copy in copies:
+        copy.wait_send()
+    keep.wait()
+
+
+def exchange(rows, collective_id):
+    count = rows.shape[0] - 1
+    return pl.pallas_call(
+        exchange_kernel,
+        out_shape=jax.ShapeDtypeStruct(rows.shape, rows.dtype),
+        in_specs=[pl.BlockSpec(memory_space=pltpu.VMEM)],
+        out_specs=pl.BlockSpec(memory_space=pltpu.VMEM),
+        scratch_shapes=[
+            pltpu.SemaphoreType.DMA((count,)),
+            pltpu.SemaphoreType.DMA((count,)),
+            pltpu.SemaphoreType.DMA,
+        ],
+        compiler_params=pltpu.CompilerParams(
+            collective_id=collective_id, has_side_effects=True
+        ),
+    )(rows)
 
 
 def attend(soft_state, queries, key_block, allowed):
@@ -79,11 +352,16 @@
     model_width = tokens.shape[1]
     group_share = HEADS // KV_HEADS
     normed = rms_scale(tokens, attn_gain).astype(jnp.bfloat16)
-    columns = normed
-    query_full = product(columns, lax.all_gather(w_query, "tok", axis=0, tiled=True))
-    keyval_full = product(columns, lax.all_gather(w_keyval, "tok", axis=0, tiled=True))
-    queries = query_full.astype(jnp.bfloat16).reshape(row_count, KV_HEADS, group_share, HEAD_DIM)
-    keyval = keyval_full.astype(jnp.bfloat16)
+    qkv_all, wo_all, pre_all, win_own, win_other, wout_own, wout_other = gather_all(
+        jnp.concatenate([w_query, w_keyval], axis=1),
+        w_output,
+        prefix_cache[0],
+        w_expert_in[0],
+        w_expert_out[0],
+    )
+    projected = product(normed, qkv_all.reshape(model_width, -1)).astype(jnp.bfloat16)
+    queries = projected[:, :model_width].reshape(row_count, KV_HEADS, group_share, HEAD_DIM)
+    keyval = projected[:, model_width:]
     position = lax.axis_index("tok")
     positions = position * row_count + jnp.arange(row_count, dtype=jnp.int32)
     req_lengths = lengths[0]
@@ -102,14 +380,14 @@
         jnp.zeros((row_count, KV_HEADS, group_share, HEAD_DIM), jnp.float32),
     )
     soft_state = attend(soft_state, queries, near_block, allowed)
-    prefix_whole = lax.all_gather(prefix_cache[0], "tok", axis=0, tiled=True)
+    prefix_whole = pre_all.reshape(-1, pre_all.shape[2])
     maxima, totals, numerators = attend(soft_state, queries, prefix_whole, None)
     attended = (
         (numerators / totals[..., None]).astype(jnp.bfloat16).reshape(row_count, HEADS * HEAD_DIM)
     )
     columns = attended
     residual = tokens.astype(jnp.float32) + product(
-        columns, lax.all_gather(w_output, "tok", axis=0, tiled=True)
+        columns, wo_all.reshape(-1, model_width)
     )
     normed2 = rms_scale(residual, moe_gain).astype(jnp.bfloat16)
     logits = product(normed2, w_router)
@@ -119,42 +397,34 @@
     picked = jnp.sum(jnp.where(expert_marks, logits[:, None, :], 0.0), axis=-1)
     scores = jax.nn.sigmoid(picked)
     gate_weights = scores / jnp.sum(scores, axis=-1, keepdims=True)
-    capacity = max(4, 5 * row_count * TOP // (4 * experts))
     flat_routes = chosen.reshape(-1)
     flat_marks = expert_marks.reshape(-1, experts).astype(jnp.int32)
     prior_count = jnp.cumsum(flat_marks, axis=0, dtype=jnp.int32) - flat_marks
     slot_index = jnp.sum(prior_count * flat_marks, axis=1)
-    target = flat_routes * capacity + slot_index
-    copies = flat_routes.shape[0]
-    slot_match = target[None, :] == jnp.arange(experts * capacity, dtype=jnp.int32)[:, None]
-    filled = jnp.any(slot_match, axis=1)
-    source = jnp.sum(jnp.where(slot_match, jnp.arange(copies, dtype=jnp.int32)[None, :], 0), axis=1)
-    outgoing = jnp.where(filled[:, None], normed2[source // TOP], 0).reshape(
-        experts, capacity, model_width
-    )
-    to_send = jnp.repeat(outgoing, 2, axis=0)
-    arrived = lax.all_to_all(to_send, "tok", split_axis=0, concat_axis=0, tiled=True)
+    target = (flat_routes * SLOTS + slot_index).reshape(row_count, TOP)
+    slot_ids = jnp.arange(experts * SLOTS, dtype=jnp.int32)
+    first, second = target[:, 0], target[:, 1]
+    place = (first[None, :] == slot_ids[:, None]) | (second[None, :] == slot_ids[:, None])
+    outgoing = product(place.astype(jnp.bfloat16), normed2).astype(jnp.bfloat16)
+    arrived = exchange(outgoing.reshape(experts, SLOTS, model_width), 1)
     flat_rows = arrived.reshape(-1, model_width)
-    columns = flat_rows
-    gate_up = product(columns, lax.all_gather(w_expert_in[0], "grp", axis=0, tiled=True))
-    half_units = gate_up.shape[1] // 2
-    act = (jax.nn.silu(gate_up[:, :half_units]) * gate_up[:, half_units:]).astype(jnp.bfloat16)
-    columns = act
-    partial_out = product(columns, lax.all_gather(w_expert_out[0], "grp", axis=0, tiled=True))
-    returned = lax.all_to_all(
-        partial_out.reshape(arrived.shape).astype(jnp.bfloat16),
-        "tok",
-        split_axis=0,
-        concat_axis=0,
-        tiled=True,
-    ).astype(jnp.float32)
-    results = jnp.sum(returned.reshape(experts, 2, capacity, model_width), axis=1).astype(
-        jnp.bfloat16
-    )
-    gathered = results.reshape(experts * capacity, model_width)[target].astype(jnp.float32)
-    weighted = jnp.sum(
-        gathered.reshape(row_count, TOP, model_width) * gate_weights[:, :, None], axis=1
-    )
+
+    def half_expert(w_in, w_out):
+        gate_up = product(flat_rows, w_in.reshape(model_width, -1))
+        half_units = gate_up.shape[1] // 2
+        act = (jax.nn.silu(gate_up[:, :half_units]) * gate_up[:, half_units:]).astype(jnp.bfloat16)
+        return product(act, w_out.reshape(half_units, model_width))
+
+    expert_out = half_expert(win_own, wout_own) + half_expert(win_other, wout_other)
+    returned = exchange(
+        expert_out.astype(jnp.bfloat16).reshape(experts, SLOTS, model_width), 2
+    )
+    results = returned.reshape(-1, model_width)
+    gates = jnp.where(first[:, None] == slot_ids[None, :], gate_weights[:, :1], 0.0)
+    gates += jnp.where(second[:, None] == slot_ids[None, :], gate_weights[:, 1:], 0.0)
+    gates_high = lax.reduce_precision(gates, exponent_bits=8, mantissa_bits=7)
+    gates_low = (gates - gates_high).astype(jnp.bfloat16)
+    weighted = product(gates_high.astype(jnp.bfloat16), results) + product(gates_low, results)
     hidden = (residual + weighted).astype(jnp.bfloat16)
     return (hidden[None], keyval[None])
 

time: 536 us -> 227 us (0.42)
  waiting for transfers between devices: 426 us -> 0.01 us
  Pallas kernels: 0 us -> 161 us
  local copies, waits for them, and re-layouts: 28.2 us -> 5.88 us
  starting transfers between devices: 18.5 us -> 2.09 us
  between operations: 14.5 us -> 1.15 us
  matrix products: 33 us -> 38.5 us
    all_gather x6 -> x0, waiting for transfers between devices: 280 us -> none  [the longest x1 65.7 us: on_device(): lax.all_gather(w_query, 'tok', axis=0, tiled=True)]
    pallas_call x0 -> x3, Pallas kernels: none -> 161 us  [the longest x2 83.4 us: exchange(): pl.pallas_call(exchange_kernel, out_shape=jax.ShapeDtypeStruct(rows.shape...]
    all_to_all x2 -> x0, waiting for transfers between devices: 142 us -> none  [the longest x1 71.3 us: on_device(): lax.all_to_all(to_send, 'tok', split_axis=0, concat_axis=0, tiled=True)]
    all_to_all x2 -> x0, starting transfers between devices: 15.4 us -> none  [the longest x1 8.96 us: on_device(): lax.all_to_all(partial_out.reshape(arrived.shape).astype(jnp.bfloat16), '...]
    convert_element_type x4 -> x0, local copies, waits for them, and re-layouts: 8 us -> none  [the longest x1 4.45 us: on_device(): partial_out.reshape(arrived.shape).astype(jnp.bfloat16)]
    gather x3 -> x0, local copies, waits for them, and re-layouts: 7.28 us -> none  [the longest x2 4.47 us: on_device(): normed2[source // TOP]]
    dot_general x2, matrix products: 3.26 us -> 10.1 us  [attend(): jnp.einsum('tkgd,skd->tkgs', queries, key_rows, preferred_element_type=jn...]
    reduce_sum x3 -> x0, other arithmetic: 6.18 us -> none  [the longest x1 3.56 us: on_device(): jnp.sum(gathered.reshape(row_count, TOP, model_width) * gate_weights[:, :...]
  transfers between devices with their start and end apart: 9 -> 1, of which waited for: 7 -> 0; matrix products, arithmetic and copies ran while one was open for 10% -> 4% of each run, Pallas kernels for 0% -> 0%
where the time goes in v1:
time: 227 us; the launch traced here: 224 us
  Pallas kernels  161 us (71%)
  matrix products  38.5 us (17%)
  other arithmetic  16.1 us (7%)
  local copies, waits for them, and re-layouts  5.88 us (3%)
    pallas_call x2, Pallas kernels, exchange(): pl.pallas_call(exchange_kernel, out_shape=jax.ShapeDtypeStruct(rows.shape...  83.4 us
    pallas_call x1, Pallas kernels, gather_all(): pl.pallas_call(gather_kernel, out_shape=[jax.ShapeDtypeStruct(shape, dtyp...  77.3 us
    dot_general x10, matrix products, product(): return jnp.dot(left, right, preferred_element_type=jnp.float32)  21.1 us
    reduce_sum x2, other arithmetic, attend(): totals = totals * rescale + jnp.sum(weights, axis=-1)  10.3 us
    dot_general x2, matrix products, attend(): jnp.einsum('tkgd,skd->tkgs', queries, key_rows, preferred_element_type=jn...  10.1 us
    dot_general x2, matrix products, attend(): jnp.einsum('tkgs,skd->tkgd', weights.astype(jnp.bfloat16), value_rows, pr...  7.41 us
  transfers between devices with their start and end apart: 1, of which 0 were waited for; matrix products, arithmetic and copies ran while one was open for 4% of the time, Pallas kernels for 0%

profile of v1, /device:TPU:1, one launch (start us, length us, event | category | flops | bytes accessed | tf_op | source)
XLA Modules:
  0.0 224.5 jit_solution(914656199489242987)
XLA Ops:
  0.6 0.0 copy-start
  0.6 0.0 copy-start.5
  0.7 1.3 fusion.23
  2.0 1.7 pad_maximum_fusion.1.qkv
  3.7 77.3 %shard_map.131 = (bf16[32,48,2560]{2,1,0:T(8,128)(2,1)}, bf16[32,48,1536]{2,1,0:T(8,128)(2,1)}, bf16[32,16,1024]{2,1,0:T(8,128)(2,1)}, bf16[8,192,1024]{2,1,0:T(...) custom-call(bf16[48,2560]{1,0:T(8,128)(2,1)} %pad_maximum_fusion.1.qkv, ...), custom_call_target="tpu_custom_call" | custom-call | tf_op jit(solution)/shard_map/pallas_call | solution.py:248
  81.0 0.0 copy-done.5
  81.0 0.0 copy-done.13
  81.0 5.0 %convolution_convert_fusion = bf16[192,2560]{1,0:T(8,128)(2,1)S(1)} fusion(bf16[1536,2560]{1,0:T(8,128)(2,1)} %bitcast.152, bf16[1,192,1536]{2,1,0:T(8,128)(2,1)S(1)} %copy-done.5, f32[1536]{0:T(1024)S(1)} %copy-done.13, f32[192]{0:T(256)S(1)} %add_rsqrt_fusion.1), kind=kOutput, calls=%fused_computation.13 | convolution fusion | flops 1511620608 | bytes 9444096 | tf_op jit(solution)/shard_map/dot_general | solution.py:40
  86.1 0.0 copy-start.8
  86.1 1.0 slice_bitcast_fusion
  87.0 2.1 collective-permute-start
  89.2 0.1 copy.51
  89.3 0.1 eq.108
  89.4 0.1 eq.112
  89.6 1.3 fusion.68
  90.9 0.0 copy-start.9
  90.9 0.0 slice-start.3
  90.9 0.2 copy.50
  91.1 0.2 copy.49
  91.3 0.6 slice-done.3
  91.9 0.3 copy.47
  92.2 0.1 copy.45
  92.3 0.1 reduce-window.18
  92.4 0.1 reduce
  92.5 0.1 pad_add_fusion.1
  92.6 0.1 convert_reduce_fusion.1
  92.7 0.9 reduce-window.19
  93.6 0.2 slice_reduce_fusion.2
  93.8 0.1 fusion.57
  93.9 0.1 reduce_sum.89
  94.1 0.2 slice_reduce_fusion.1
  94.3 0.1 copy.55
  94.4 0.1 pad_add_fusion
  94.5 0.1 compare_and_fusion
  94.6 5.1 %bitcast_reduce_fusion = (f32[192,8,3]{0,2,1:T(4,128)S(1)}, f32[8,512,192,3]{1,2,3,0:T(8,128)}) fusion(bf16[512,8,64,1]{0,2,3,1:T(8,128)(2,1)S(1)} %bitcast.136, bf16[192,8,3,64]{0,3,2,1:T(8,128)(2,1)S(1)} %bitcast.131), kind=kOutput, calls=%fused_computation.1 | convolution fusion | flops 306703872 | bytes 10569728 | tf_op jit(solution)/shard_map/tkgd,skd->tkgs/dot_general | solution.py:318
  99.7 0.0 collective-permute-done
  99.7 1.1 pad_maximum_fusion
  100.8 0.2 copy.46
  101.0 0.0 slice-start
  101.0 0.0 slice-start.1
  101.0 5.0 %fusion.5 = (f32[192,8,3]{0,2,1:T(4,128)S(1)}, f32[8,384,192,3]{1,2,3,0:T(8,128)}) fusion(pred[192,384]{1,0:T(8,128)(4,1)S(1)} %compare_and_fusion, bf16[384,8,64,1]{0,2,3,1:T(8,128)(2,1)S(1)} %bitcast.137, bf16[192,8,3,64]{0,3,2,1:T(8,128)(2,1)S(1)} %bitcast.132), kind=kOutput, calls=%fused_computation.9 | convolution fusion | flops 231796224 | bytes 8153088 | tf_op jit(solution)/shard_map/tkgd,skd->tkgs/dot_general | solution.py:318
  106.0 0.0 slice-start.2
  106.0 5.5 %fusion.1 = f32[192,8,3]{0,2,1:T(4,128)S(1)} fusion(f32[8,512,192,3]{1,2,3,0:T(8,128)} %get-tuple-element.34, f32[192,8,3]{0,2,1:T(4,128)S(1)} %max.13), kind=kLoop, calls=%fused_computation.3 | loop fusion | flops 7073280 | bytes 9474048 | tf_op jit(solution)/shard_map/reduce_sum | solution.py:326
  111.6 3.2 %fusion.6 = f32[8,64,192,3]{2,1,3,0:T(8,128)} fusion(bf16[512,8,64,1]{0,2,3,1:T(8,128)(2,1)S(1)} %bitcast.135, f32[8,512,192,3]{1,2,3,0:T(8,128)S(1)} %bitcast.128, f32[192,8,3]{0,2,1:T(4,128)S(1)} %max.13), kind=kOutput, calls=%fused_computation.10 | convolution fusion | flops 309067776 | bytes 11159552 | tf_op jit(solution)/shard_map/tkgs,skd->tkgd/dot_general | solution.py:327
  114.9 0.2 copy.48
  115.1 0.0 copy-start.1
  115.1 0.0 slice-start.4
  115.1 4.7 %fusion.3 = f32[192,8,3]{0,2,1:T(4,128)S(1)} fusion(f32[8,384,192,3]{1,2,3,0:T(8,128)} %get-tuple-element.32, f32[192,8,3]{0,2,1:T(4,128)S(1)} %get-tuple-element.31, pred[192,384]{1,0:T(8,128)(4,1)S(1)} %compare_and_fusion), kind=kLoop, calls=%fused_computation.7 | loop fusion | flops 7073280 | bytes 7188480 | tf_op jit(solution)/shard_map/reduce_sum | solution.py:326
  119.9 0.3 copy-done.1
  120.2 4.2 %fusion.18 = bf16[192,8,3,64]{0,3,2,1:T(8,128)(2,1)S(1)} fusion(f32[8,64,192,3]{2,1,3,0:T(8,128)} %fusion.6, bf16[384,8,64,1]{0,2,3,1:T(8,128)(2,1)S(1)} %bitcast.142, f32[8,384,192,3]{1,2,3,0:T(8,128)S(1)} %copy-done.1, f32[192,8,3]{0,2,1:T(4,128)S(1)} %get-tuple-element.31, pred[192,384]{1,0:T(8,128)(4,1)S(1)} %compare_and_fusion, ...), kind=kOutput, calls=%fused_computation.26 | convolution fusion | flops 235044864 | bytes 9388032 | tf_op jit(solution)/shard_map/tkgs,skd->tkgd/dot_general | solution.py:327
  124.4 0.0 copy-start.7
  124.4 1.2 multiply_reduce_fusion
  125.6 1.8 convolution_convert_fusion.1
  127.4 40.9 %shard_map.132 = bf16[16,32,1536]{2,1,0:T(8,128)(2,1)} custom-call(bf16[16,32,1536]{2,1,0:T(8,128)(2,1)} %bitcast.133), custom_call_target="tpu_custom_call" | custom-call | tf_op jit(solution)/shard_map/pallas_call | solution.py:293
  168.4 4.3 %fusion.70 = f32[512,1024]{1,0:T(8,128)S(1)} fusion(bf16[512,1536]{1,0:T(8,128)(2,1)} %bitcast.138, bf16[1536,1024]{1,0:T(8,128)(2,1)} %bitcast.157), kind=kOutput, calls=%fused_computation.115 | convolution fusion | flops 1610612736 | bytes 6815744 | tf_op jit(solution)/shard_map/dot_general | solution.py:40
  172.7 0.0 copy-done.4
  172.7 1.8 fusion.71
  174.5 1.0 fusion.32
  175.6 0.4 copy-done.11
  175.9 2.2 fusion.13
  178.1 42.5 %shard_map.133 = bf16[16,32,1536]{2,1,0:T(8,128)(2,1)} custom-call(bf16[16,32,1536]{2,1,0:T(8,128)(2,1)} %bitcast.140), custom_call_target="tpu_custom_call" | custom-call | tf_op jit(solution)/shard_map/pallas_call | solution.py:293
  220.6 0.3 fusion.67
  221.0 2.0 fusion.44
  223.1 1.4 fusion.16
  (38 shorter events, 0.3 us)
Async XLA Ops:
  0.6 220.0 %copy-start = (bf16[1536,16]{0,1:T(8,128)(2,1)S(1)}, bf16[1536,16]{0,1:T(8,128)(2,1)}, u32[]{:S(2)}) copy-start(bf16[1536,16]{0,1:T(8,128)(2,1)} %param.20) | copy-start | bytes 147460
  0.6 80.4 %copy-start.5 = (bf16[1,192,1536]{2,1,0:T(8,128)(2,1)S(1)}, bf16[1,192,1536]{2,1,0:T(8,128)(2,1)}, u32[]{:S(2)}) copy-start(bf16[1,192,1536]{2,1,0:T(8,128)(2,1)} %param.12) | copy-start | bytes 1769476
  0.7 80.4 %copy-start.13 = (f32[1536]{0:T(1024)S(1)}, f32[1536]{0:T(1024)}, u32[]{:S(2)}) copy-start(f32[1536]{0:T(1024)} %param.13) | copy-start | bytes 18436
  86.0 4.8 %copy-start.3 = (bf16[192,2560]{1,0:T(8,128)(2,1)}, bf16[192,2560]{1,0:T(8,128)(2,1)S(1)}, u32[]{:S(2)}) copy-start(bf16[192,2560]{1,0:T(8,128)(2,1)S(1)} %convolution_convert_fusion) | copy-start | bytes 2949124
  86.1 3.1 %copy-start.8 = (s32[1,192,2]{1,2,0:T(2,128)S(1)}, s32[1,192,2]{1,2,0:T(2,128)}, u32[]{:S(2)}) copy-start(s32[1,192,2]{1,2,0:T(2,128)} %param.21) | copy-start | bytes 4612
  87.0 12.7 %collective-permute-start = (bf16[192,1024]{1,0:T(8,128)(2,1)S(1)}, bf16[192,1024]{1,0:T(8,128)(2,1)}, u32[]{:S(2)}, u32[]{:S(2)}) collective-permute-start(bf16[192,1024]{1,0:T(8,128)(2,1)S(1)} %get-tuple-element.25), channel_id=1, source_target_pairs={{0,1},{1,2},{2,3},{3,4},{4,5},{5,6},{6,7},{7,8},{8,9},{9,10},{10,1... | collective-permute-start | bytes 1179656 | tf_op jit(solution)/shard_map/ppermute | solution.py:25
  90.9 1.4 copy-start.9
  90.9 1.1 slice-start.3
  101.0 10.6 %slice-start = ((s8[9437184]{0:T(1024)(128)(4,1)}), s8[4194304]{0:T(1024)(128)(4,1)S(1)}, s32[]{:S(2)}) async-start(s8[9437184]{0:T(1024)(128)(4,1)} %bitcast.127), calls=%async_computation | async-start | bytes 8388608
  101.0 10.6 %slice-start.1 = ((s8[9437184]{0:T(1024)(128)(4,1)}), s8[4194304]{0:T(1024)(128)(4,1)S(1)}, s32[]{:S(2)}) async-start(s8[9437184]{0:T(1024)(128)(4,1)} %bitcast.127), calls=%async_computation.1 | async-start | bytes 8388608
  106.0 5.6 %slice-start.2 = ((s8[9437184]{0:T(1024)(128)(4,1)}), s8[1048576]{0:T(1024)(128)(4,1)S(1)}, s32[]{:S(2)}) async-start(s8[9437184]{0:T(1024)(128)(4,1)} %bitcast.127), calls=%async_computation.2 | async-start | bytes 2097152
  115.1 5.1 %copy-start.1 = (f32[8,384,192,3]{1,2,3,0:T(8,128)S(1)}, f32[8,384,192,3]{1,2,3,0:T(8,128)}, u32[]{:S(2)}) copy-start(f32[8,384,192,3]{1,2,3,0:T(8,128)} %get-tuple-element.32) | copy-start | bytes 21233668
  115.1 9.2 %slice-start.4 = ((s8[4718592]{0:T(1024)(128)(4,1)}), s8[4194304]{0:T(1024)(128)(4,1)S(1)}, s32[]{:S(2)}) async-start(s8[4718592]{0:T(1024)(128)(4,1)} %bitcast.153), calls=%async_computation.4 | async-start | bytes 8388608
  120.2 4.2 %copy-start.6 = (bf16[1,192,1536]{2,1,0:T(8,128)(2,1)S(1)}, bf16[1,192,1536]{2,1,0:T(8,128)(2,1)}, u32[]{:S(2)}) copy-start(bf16[1,192,1536]{2,1,0:T(8,128)(2,1)} %param.12) | copy-start | bytes 1769476
  120.2 4.2 %slice-start.5 = ((s8[4718592]{0:T(1024)(128)(4,1)}), s8[524288]{0:T(1024)(128)(4,1)S(1)}, s32[]{:S(2)}) async-start(s8[4718592]{0:T(1024)(128)(4,1)} %bitcast.153), calls=%async_computation.5 | async-start | bytes 1048576
  124.4 1.2 copy-start.7
  168.4 4.3 %copy-start.4 = (bf16[16,32,1536]{2,1,0:T(8,128)(2,1)S(1)}, bf16[16,32,1536]{2,1,0:T(8,128)(2,1)}, u32[]{:S(2)}) copy-start(bf16[16,32,1536]{2,1,0:T(8,128)(2,1)} %shard_map.132) | copy-start | bytes 4718596
  168.4 4.3 %copy-start.10 = (bf16[8,192,1024]{2,1,0:T(8,128)(2,1)S(1)}, bf16[8,192,1024]{2,1,0:T(8,128)(2,1)}, u32[]{:S(2)}) copy-start(bf16[8,192,1024]{2,1,0:T(8,128)(2,1)} %get-tuple-element.14) | copy-start | bytes 9437188
  172.7 1.8 copy-start.12
  174.5 1.4 copy-start.11
  220.6 2.4 %copy-start.2 = (bf16[16,32,1536]{2,1,0:T(8,128)(2,1)S(1)}, bf16[16,32,1536]{2,1,0:T(8,128)(2,1)}, u32[]{:S(2)}) copy-start(bf16[16,32,1536]{2,1,0:T(8,128)(2,1)} %shard_map.133) | copy-start | bytes 4718596
